TPU v7x, 32 devices: a whole 2x2x4 slice. The times are simulated.
32 devices in a mesh: seq: 8 (over z, x), head: 4 (over y, core).
Axes of the slice: x: 2, y: 2, z: 4, core: 2. Of those that a mesh axis runs over, the one named last changes fastest.
Arguments:
- features: bfloat16 [8192, 8192], P(('seq', 'head')), may hold values from -6 to 6
- gate_input: bfloat16 [8192, 8192], P(('seq', 'head')), may hold values from -6 to 6
- bmat: bfloat16 [8192, 8, 128], P(('seq', 'head')), may hold values from -1.78125 to 1.78125
- cmat: bfloat16 [8192, 8, 128], P(('seq', 'head')), may hold values from -1.78125 to 1.78125
- step_size: float32 [8192, 128], P(('seq', 'head')), may hold values from 0.001 to 0.1
- log_decay: float32 [8192, 128], P(('seq', 'head')), may hold values from -0.8 to 0
- skip: float32 [128], P('head'), may hold values from 0.5 to 2
- norm_gain: float32 [8192], replicated, may hold values from 0.1 to 1.9
Outputs:
- mixed: bfloat16 [8192, 8192], P(('seq', 'head'))
All inputs are finite; a program needn't handle non-finite values.
Results may differ from a plain program's by a relative error of at most 0.0085.
Values may be sent and summed in bfloat16 or wider, within the bound.
No kernel may reach another device: no remote copies, remote signals or barrier semaphores. Data moves between devices by JAX's collectives and lax.ppermute only.
A program may use at most 128 MiB of HBM per device.

v0:
```python
import jax
import jax.numpy as jnp
from jax import lax
from jax.sharding import PartitionSpec as P

SPAN = 256


def passed_along(value, axis, steps):
    count = lax.axis_size(axis)
    leading, last = (max(0, -steps), min(count, count - steps))
    return lax.ppermute(value, axis, [(source, source + steps) for source in range(leading, last)])


def block_terms(feature_block, b_block, c_block, dt_block, cum_block):
    length = cum_block.shape[0]
    token_positions = jnp.arange(length)
    causal = token_positions[:, None] >= token_positions[None, :]
    scores = jnp.einsum("tgn,sgn->gts", c_block, b_block, preferred_element_type=jnp.float32)
    cum_heads = jnp.transpose(cum_block, (1, 2, 0))
    spread = cum_heads[:, :, :, None] - cum_heads[:, :, None, :]
    step_scale = jnp.transpose(dt_block, (1, 2, 0))[:, :, None, :]
    weights = jnp.where(
        causal, scores[:, None] * jnp.exp(jnp.where(causal, spread, 0.0)) * step_scale, 0.0
    ).astype(jnp.bfloat16)
    intra_terms = jnp.einsum(
        "ghts,sghp->tghp", weights, feature_block, preferred_element_type=jnp.float32
    )
    tail_scale = jnp.exp(cum_block[-1:] - cum_block) * dt_block
    loaded = (b_block[:, :, None, :].astype(jnp.float32) * tail_scale[..., None]).astype(
        jnp.bfloat16
    )
    update = jnp.einsum(
        "sghn,sghp->ghpn", loaded, feature_block, preferred_element_type=jnp.float32
    )
    return (intra_terms, update)


def normalize(values, gate_part, gain_row):
    gated_values = values.astype(jnp.float32) * jax.nn.silu(gate_part.astype(jnp.float32))
    inverse_rms = lax.rsqrt(jnp.mean(gated_values * gated_values, axis=-1, keepdims=True) + 1e-05)
    return (gated_values * inverse_rms * gain_row).astype(jnp.bfloat16)


def pair_terms(members):
    return jax.vmap(block_terms)(*members)


def shards(features, gate_input, bmat, cmat, step_size, log_decay, skip, norm_gain):
    tok_rows = features.shape[0]
    group_count = bmat.shape[1]
    state_size = bmat.shape[2]
    heads_total = step_size.shape[1]
    per_group = heads_total // group_count
    group_width = features.shape[1] // group_count
    head_size = group_width // per_group
    feature_groups = features.reshape(tok_rows, group_count, group_width)
    gate_groups = gate_input.reshape(tok_rows, group_count, group_width)
    dt_groups = step_size.reshape(tok_rows, group_count, per_group)
    decay_groups = log_decay.reshape(tok_rows, group_count, per_group)
    feature_here, gate_here, b_here, c_here = (
        lax.all_to_all(feature_groups, "head", split_axis=1, concat_axis=0, tiled=True),
        lax.all_to_all(gate_groups, "head", split_axis=1, concat_axis=0, tiled=True),
        lax.all_to_all(bmat, "head", split_axis=1, concat_axis=0, tiled=True),
        lax.all_to_all(cmat, "head", split_axis=1, concat_axis=0, tiled=True),
    )
    dt_here, decay_here = (
        lax.all_to_all(dt_groups, "head", split_axis=1, concat_axis=0, tiled=True),
        lax.all_to_all(decay_groups, "head", split_axis=1, concat_axis=0, tiled=True),
    )
    seq_rows = feature_here.shape[0]
    local_groups = feature_here.shape[1]
    blocks = seq_rows // SPAN
    feature_blocks = feature_here.reshape(blocks, SPAN, local_groups, per_group, head_size)
    b_blocks = b_here.reshape(blocks, SPAN, local_groups, state_size)
    c_blocks = c_here.reshape(blocks, SPAN, local_groups, state_size)
    dt_blocks = dt_here.reshape(blocks, SPAN, local_groups, per_group)
    decay_blocks = decay_here.reshape(blocks, SPAN, local_groups, per_group)
    cum_blocks = jnp.cumsum(decay_blocks, axis=1)

    def paired(array):
        return array.reshape((blocks // 2, 2) + array.shape[1:])

    intra_terms, updates = lax.map(
        pair_terms,
        (
            paired(feature_blocks),
            paired(b_blocks),
            paired(c_blocks),
            paired(dt_blocks),
            paired(cum_blocks),
        ),
    )
    intra_terms = intra_terms.reshape(blocks, SPAN, local_groups, per_group, head_size)
    updates = updates.reshape(blocks, local_groups, per_group, head_size, state_size)
    block_decay = jnp.exp(cum_blocks[:, -1])

    def advance(carry_state, members):
        decay_now, update_now = members
        return (decay_now[..., None, None] * carry_state + update_now, carry_state)

    start_state = jnp.zeros((local_groups, per_group, head_size, state_size), jnp.float32)
    local_end, local_states = lax.scan(advance, start_state, (block_decay, updates))
    block_sums = jnp.sum(decay_blocks, axis=1)
    before = jnp.cumsum(block_sums, axis=0) - block_sums
    shard_decay = jnp.exp(jnp.sum(block_sums, axis=0))

    def hop(iteration, incoming):
        return passed_along(shard_decay[..., None, None] * incoming + local_end, "seq", 1)

    entering = lax.fori_loop(0, lax.axis_size("seq") - 1, hop, jnp.zeros_like(local_end))
    states = local_states + jnp.exp(before)[..., None, None] * entering[None]
    carried = (
        jnp.einsum(
            "ktgn,kghpn->ktghp",
            c_blocks.astype(jnp.float32),
            states,
            precision=lax.Precision.HIGHEST,
        )
        * jnp.exp(cum_blocks)[..., None]
    )
    head_skip = skip.reshape(local_groups, per_group)
    ssm_out = (
        intra_terms
        + carried
        + head_skip[None, None, :, :, None] * feature_blocks.astype(jnp.float32)
    ).astype(jnp.bfloat16)
    ssm_out = ssm_out.reshape(seq_rows, local_groups, group_width)
    offset = lax.axis_index("head") * (local_groups * group_width)
    gain_here = lax.dynamic_slice_in_dim(norm_gain, offset, local_groups * group_width).reshape(
        local_groups, group_width
    )
    mixed_here = normalize(ssm_out, gate_here, gain_here)
    restored = lax.all_to_all(mixed_here, "head", split_axis=0, concat_axis=1, tiled=True)
    return restored.reshape(tok_rows, features.shape[1])


def solution(mesh):
    return jax.shard_map(
        shards,
        mesh=mesh,
        in_specs=(
            P(("seq", "head"), None),
            P(("seq", "head"), None),
            P(("seq", "head"), None, None),
            P(("seq", "head"), None, None),
            P(("seq", "head"), None),
            P(("seq", "head"), None),
            P("head"),
            P(),
        ),
        out_specs=P(("seq", "head"), None),
        check_vma=False,
    )
```

profile of v0, /device:TPU:31, one launch (start us, length us, event | category | flops | bytes accessed | tf_op | source)
XLA Modules:
  0.0 474.6 jit_solution(16098080593060179614)
XLA Ops:
  0.0 1.7 copy.123
  1.7 4.1 all-to-all-start.3
  5.7 1.6 copy.128
  8.5 5.1 %all-to-all-start.4 = ((f32[256,8,16]{0,2,1:T(8,128)}), f32[256,8,16]{0,2,1:T(8,128)S(1)}, u32[]{:S(2)}, u32[]{:S(2)}) async-start(f32[256,8,16]{0,2,1:T(8,128)} %bitcast.28), calls=%async_computation.4 | async-start | bytes 262144 | tf_op jit(solution)/shard_map/all_to_all | solution.py:68
  13.6 1.9 copy.121
  16.4 5.9 %all-to-all-start.1 = ((bf16[256,8,128]{2,0,1:T(8,128)(2,1)}), bf16[256,8,128]{2,0,1:T(8,128)(2,1)}, u32[]{:S(2)}, u32[]{:S(2)}) async-start(bf16[256,8,128]{2,0,1:T(8,128)(2,1)} %copy.121), calls=%async_computation.1 | async-start | bytes 1048576 | tf_op jit(solution)/shard_map/all_to_all | solution.py:65
  22.3 6.4 %copy.118 = bf16[256,8192]{0,1:T(8,128)(2,1)} copy(bf16[256,8192]{1,0:T(8,128)(2,1)} %param.14) | data formatting | bytes 8388608 | tf_op args[0]
  28.7 6.5 %copy.119 = bf16[256,8,1024]{2,0,1:T(8,128)(2,1)} copy(bf16[256,8,1024]{0,2,1:T(8,128)(2,1)} %bitcast.164) | data formatting | bytes 8388608 | tf_op jit(solution)/shard_map/reshape | solution.py:57
  35.3 5.0 %all-to-all-start = ((bf16[256,8,1024]{2,0,1:T(8,128)(2,1)}), bf16[256,8,1024]{2,0,1:T(8,128)(2,1)}, u32[]{:S(2)}, u32[]{:S(2)}) async-start(bf16[256,8,1024]{2,0,1:T(8,128)(2,1)} %copy.119), calls=%async_computation | async-start | bytes 8388608 | tf_op jit(solution)/shard_map/all_to_all | solution.py:62
  41.2 6.4 %copy.132 = bf16[256,8192]{0,1:T(8,128)(2,1)} copy(bf16[256,8192]{1,0:T(8,128)(2,1)} %param.15) | data formatting | bytes 8388608 | tf_op args[1]
  48.9 4.6 reduce-window.6
  54.0 32.7 %all-to-all-done = bf16[256,8,1024]{2,0,1:T(8,128)(2,1)} async-done(((bf16[256,8,1024]{2,0,1:T(8,128)(2,1)}), bf16[256,8,1024]{2,0,1:T(8,128)(2,1)}, u32[]{:S(2)}, u32[]{:S(2)}) %all-to-all-start) | async-done | bytes 4194336 | tf_op jit(solution)/shard_map/all_to_all | solution.py:62
  86.7 5.3 %all-to-all-start.2 = ((bf16[256,8,128]{2,0,1:T(8,128)(2,1)}), bf16[256,8,128]{2,0,1:T(8,128)(2,1)S(1)}, u32[]{:S(2)}, u32[]{:S(2)}) async-start(bf16[256,8,128]{2,0,1:T(8,128)(2,1)} %copy.122), calls=%async_computation.2 | async-start | bytes 1048576 | tf_op jit(solution)/shard_map/all_to_all | solution.py:64
  92.3 6.2 %copy.120 = bf16[256,4,2,1024]{0,3,2,1:T(8,128)(2,1)} copy(bf16[256,4,2,1024]{3,0,2,1:T(8,128)(2,1)} %bitcast.13) | data formatting | bytes 8388608 | tf_op jit(solution)/shard_map/all_to_all | solution.py:62
  98.9 6.7 %all-to-all-start.5 = ((bf16[256,8,1024]{0,2,1:T(8,128)(2,1)}), bf16[256,8,1024]{0,2,1:T(8,128)(2,1)}, u32[]{:S(2)}, u32[]{:S(2)}) async-start(bf16[256,8,1024]{0,2,1:T(8,128)(2,1)} %bitcast.161), calls=%async_computation.5 | async-start | bytes 8388608 | tf_op jit(solution)/shard_map/all_to_all | solution.py:63
  105.6 31.4 %while.35 = (s32[]{:T(128)}, f32[2,2,256,2,16,64]{2,5,4,3,1,0:T(8,128)}, f32[2,2,2,16,64,128]{5,4,3,2,1,0:T(8,128)}, bf16[2,2,256,2,16,64]{2,5,4,3,1,0:T(8,128)(...) while((s32[]{:T(128)}, ...), condition=%wide.region_3.4_spmd, body=%wide.region_2.3_spmd.sunk | while | flops 902004736 | bytes 15929189 | solution.py:84
  108.1 7.3 %bitcast_dynamic-update-slice_fusion.6 = f32[2,2,256,2,16,64]{2,5,4,3,1,0:T(8,128)} fusion(f32[2,2,256,2,16,64]{2,5,4,3,1,0:T(8,128)} %get-tuple-element.328, s32[]{:T(128)} %get-tuple-element.327, f32[2,2,16,256]{3,2,1,0:T(8,128)S(1)} %copy.162, f32[2,2,16,256]{3,2,1,0:T(8,128)S(1)} %copy.164, f32[2,2,256,256]{3,2,1,0:T(8,128)S(1)} %fusion.52, ...), kind=kOutput, calls=%fused_computation.10.clone.1 | convolution fusion | flops 562036736 | bytes 7603200 | tf_op jit(solution)/shard_map/while/body/eval_jaxpr/vmap(ghts,sghp->tghp)/dot_general | solution.py:26
  116.1 5.1 %bitcast_dynamic-update-slice_fusion.7 = f32[2,2,2,16,64,128]{5,4,3,2,1,0:T(8,128)} fusion(f32[2,2,2,16,64,128]{5,4,3,2,1,0:T(8,128)} %get-tuple-element.329, s32[]{:T(128)} %get-tuple-element.327, f32[2,256,2,16]{1,3,2,0:T(8,128)S(1)} %copy.165, f32[2,256,2,128]{3,1,2,0:T(8,128)S(1)} %bitcast_convert_fusion.2, ...), kind=kOutput, calls=%fused_computation.13.clone.1 | convolution fusion | flops 272629760 | bytes 4785152 | tf_op jit(solution)/shard_map/while/body/eval_jaxpr/vmap(sghn,sghp->ghpn)/dot_general | solution.py:33
  123.8 7.3 %bitcast_dynamic-update-slice_fusion.6 = f32[2,2,256,2,16,64]{2,5,4,3,1,0:T(8,128)} fusion(f32[2,2,256,2,16,64]{2,5,4,3,1,0:T(8,128)} %get-tuple-element.328, s32[]{:T(128)} %get-tuple-element.327, f32[2,2,16,256]{3,2,1,0:T(8,128)S(1)} %copy.162, f32[2,2,16,256]{3,2,1,0:T(8,128)S(1)} %copy.164, f32[2,2,256,256]{3,2,1,0:T(8,128)S(1)} %fusion.52, ...), kind=kOutput, calls=%fused_computation.10.clone.1 | convolution fusion | flops 562036736 | bytes 7603200 | tf_op jit(solution)/shard_map/while/body/eval_jaxpr/vmap(ghts,sghp->tghp)/dot_general | solution.py:26
  131.9 5.1 %bitcast_dynamic-update-slice_fusion.7 = f32[2,2,2,16,64,128]{5,4,3,2,1,0:T(8,128)} fusion(f32[2,2,2,16,64,128]{5,4,3,2,1,0:T(8,128)} %get-tuple-element.329, s32[]{:T(128)} %get-tuple-element.327, f32[2,256,2,16]{1,3,2,0:T(8,128)S(1)} %copy.165, f32[2,256,2,128]{3,1,2,0:T(8,128)S(1)} %bitcast_convert_fusion.2, ...), kind=kOutput, calls=%fused_computation.13.clone.1 | convolution fusion | flops 272629760 | bytes 4785152 | tf_op jit(solution)/shard_map/while/body/eval_jaxpr/vmap(sghn,sghp->ghpn)/dot_general | solution.py:33
  137.0 10.0 %while.37 = (s32[]{:T(128)}, f32[2,16,64,128]{3,2,1,0:T(8,128)S(1)}, f32[4,2,16,64,128]{4,3,2,1,0:T(8,128)}, f32[4,2,16]{2,1,0:T(2,128)S(1)}, f32[4,2,16,64,128]{4,3,2,1,0:T(8,128)}, /*index=5*/s32[]{:T(128)}, s32[]{:T(128)}) while((s32[]{:T(128)}, f32[2,16,64,128]{3,2,1,0:T(8,128)S(1)}, f32[4,2,16,64,128]{4,3,2,1,0:T(8,128)}, ...), condition=%wide.region_5.6_spmd.clone, body=%wide.region_4.5_spmd.clone.sunk | while | flops 1048579 | bytes 5243872 | solution.py:103
  138.1 1.4 bitcast_add_fusion.2
  140.6 1.4 bitcast_add_fusion.2
  143.1 1.4 bitcast_add_fusion.2
  145.6 1.4 bitcast_add_fusion.2
  147.0 4.8 %all-to-all-done.5 = bf16[256,8,1024]{0,2,1:T(8,128)(2,1)} async-done(((bf16[256,8,1024]{0,2,1:T(8,128)(2,1)}), bf16[256,8,1024]{0,2,1:T(8,128)(2,1)}, u32[]{:S(2)}, u32[]{:S(2)}) %all-to-all-start.5) | async-done | bytes 4194336 | tf_op jit(solution)/shard_map/all_to_all | solution.py:63
  151.8 6.2 %convert_element_type.75 = f32[256,8,1024]{0,2,1:T(8,128)} convert(bf16[256,8,1024]{0,2,1:T(8,128)(2,1)} %all-to-all-done.5) | non-fusion elementwise | flops 2097152 | bytes 12582912 | tf_op jit(solution)/shard_map/convert_element_type | solution.py:40
  158.1 168.5 %while.36 = (s32[]{:T(128)}, f32[2,16,64,128]{3,2,1,0:T(8,128)S(1)}, f32[2,16]{1,0:T(2,128)S(1)}, f32[2,16,64,128]{3,2,1,0:T(8,128)S(1)}, s32[]{:T(128)}) while((s32[]{:T(128)}, f32[2,16,64,128]{3,2,1,0:T(8,128)S(1)}, f32[2,16]{1,0:T(2,128)S(1)}, f32[2,16,64,128]{3,2,1,0:T(8,128)S(1)}, s32[]{:T(128)}) %tuple.65), condition=%wide.region_10.11_spmd, body=%wide.region_9.10_spmd.sunk | while | flops 524290 | bytes 7340261 | solution.py:111
  159.6 24.5 %collective-permute-done = f32[2,16,64,128]{3,2,1,0:T(8,128)S(1)} collective-permute-done((f32[2,16,64,128]{3,2,1,0:T(8,128)S(1)}, f32[2,16,64,128]{3,2,1,0:T(8,128)S(1)}, u32[]{:S(2)}, u32[]{:S(2)}) %collective-permute-start) | collective-permute-done | bytes 1048608 | tf_op jit(solution)/shard_map/while/body/eval_jaxpr/ppermute | solution.py:12
  184.2 1.3 collective-permute-start
  185.5 23.7 %collective-permute-done = f32[2,16,64,128]{3,2,1,0:T(8,128)S(1)} collective-permute-done((f32[2,16,64,128]{3,2,1,0:T(8,128)S(1)}, f32[2,16,64,128]{3,2,1,0:T(8,128)S(1)}, u32[]{:S(2)}, u32[]{:S(2)}) %collective-permute-start) | collective-permute-done | bytes 1048608 | tf_op jit(solution)/shard_map/while/body/eval_jaxpr/ppermute | solution.py:12
  210.7 23.7 %collective-permute-done = f32[2,16,64,128]{3,2,1,0:T(8,128)S(1)} collective-permute-done((f32[2,16,64,128]{3,2,1,0:T(8,128)S(1)}, f32[2,16,64,128]{3,2,1,0:T(8,128)S(1)}, u32[]{:S(2)}, u32[]{:S(2)}) %collective-permute-start) | collective-permute-done | bytes 1048608 | tf_op jit(solution)/shard_map/while/body/eval_jaxpr/ppermute | solution.py:12
  235.8 22.9 %collective-permute-done = f32[2,16,64,128]{3,2,1,0:T(8,128)S(1)} collective-permute-done((f32[2,16,64,128]{3,2,1,0:T(8,128)S(1)}, f32[2,16,64,128]{3,2,1,0:T(8,128)S(1)}, u32[]{:S(2)}, u32[]{:S(2)}) %collective-permute-start) | collective-permute-done | bytes 1048608 | tf_op jit(solution)/shard_map/while/body/eval_jaxpr/ppermute | solution.py:12
  260.2 22.0 %collective-permute-done = f32[2,16,64,128]{3,2,1,0:T(8,128)S(1)} collective-permute-done((f32[2,16,64,128]{3,2,1,0:T(8,128)S(1)}, f32[2,16,64,128]{3,2,1,0:T(8,128)S(1)}, u32[]{:S(2)}, u32[]{:S(2)}) %collective-permute-start) | collective-permute-done | bytes 1048608 | tf_op jit(solution)/shard_map/while/body/eval_jaxpr/ppermute | solution.py:12
  282.3 1.3 collective-permute-start
  283.6 21.1 %collective-permute-done = f32[2,16,64,128]{3,2,1,0:T(8,128)S(1)} collective-permute-done((f32[2,16,64,128]{3,2,1,0:T(8,128)S(1)}, f32[2,16,64,128]{3,2,1,0:T(8,128)S(1)}, u32[]{:S(2)}, u32[]{:S(2)}) %collective-permute-start) | collective-permute-done | bytes 1048608 | tf_op jit(solution)/shard_map/while/body/eval_jaxpr/ppermute | solution.py:12
  306.3 20.3 %collective-permute-done = f32[2,16,64,128]{3,2,1,0:T(8,128)S(1)} collective-permute-done((f32[2,16,64,128]{3,2,1,0:T(8,128)S(1)}, f32[2,16,64,128]{3,2,1,0:T(8,128)S(1)}, u32[]{:S(2)}, u32[]{:S(2)}) %collective-permute-start) | collective-permute-done | bytes 1048608 | tf_op jit(solution)/shard_map/while/body/eval_jaxpr/ppermute | solution.py:12
  326.5 13.8 %multiply_reduce_fusion = (f32[4,256,2]{1,2,0:T(2,128)S(1)}, f32[4,256,2,16,64]{1,4,3,2,0:T(8,128)}) fusion(f32[4,256,2,16,64]{1,4,3,2,0:T(8,128)} %bitcast.157, bf16[4,256,2,16,64]{1,4,3,2,0:T(8,128)(2,1)} %bitcast.167, f32[2,16]{1,0:T(2,128)S(1)} %mul.128, f32[4,256,2,16]{1,3,2,0:T(8,128)S(1)} %bitcast_exponential_fusion, ...), kind=kOutput, calls=%fused_computation.43 | convolution fusion | flops 3252680704 | bytes 35267200 | tf_op jit(solution)/shard_map/ktgn,kghpn->ktghp/dot_general | solution.py:114
  340.3 13.8 %copy.131 = f32[4,256,2,16,64]{1,0,4,3,2:T(4,128)} copy(f32[4,256,2,16,64]{1,4,3,2,0:T(8,128)} %get-tuple-element.208) | data formatting | bytes 16777216 | tf_op jit(solution)/shard_map/convert_element_type | solution.py:40
  354.1 10.7 %reshape.131 = f32[1024,2,1024]{0,2,1:T(8,128)} reshape(f32[4,256,2,16,64]{1,0,4,3,2:T(4,128)} %copy.131) | data formatting | bytes 16777216 | tf_op jit(solution)/shard_map/convert_element_type | solution.py:40
  364.9 8.8 %copy.134 = f32[4,256,2,1024]{3,1,0,2:T(8,128)} copy(f32[4,256,2,1024]{1,3,2,0:T(8,128)} %bitcast.158) | data formatting | bytes 16777216 | tf_op jit(solution)/shard_map/convert_element_type | solution.py:40
  373.6 8.7 %copy.136 = f32[1024,2,1024]{0,2,1:T(8,128)} copy(f32[1024,2,1024]{2,0,1:T(8,128)} %bitcast.159) | data formatting | bytes 16777216 | tf_op jit(solution)/shard_map/convert_element_type | solution.py:40
  382.3 8.6 %multiply_convert_fusion.4 = bf16[1024,2,1024]{0,2,1:T(8,128)(2,1)} fusion(f32[1024,2,1024]{0,2,1:T(8,128)} %reshape.131, f32[1024,2,1024]{0,2,1:T(8,128)} %copy.136, f32[2,1024]{1,0:T(2,128)S(1)} %copy-done.1, f32[1024,2]{0,1:T(2,128)S(1)} %bitcast.174), kind=kLoop, calls=%fused_computation.42 | loop fusion | flops 16777216 | bytes 20987904 | tf_op jit(solution)/shard_map/convert_element_type | solution.py:42
  390.9 11.3 %copy.138 = bf16[1024,2,1024]{2,1,0:T(2,128)(2,1)} copy(bf16[1024,2,1024]{0,2,1:T(8,128)(2,1)} %multiply_convert_fusion.4) | data formatting | bytes 8388608 | tf_op jit(solution)/shard_map/convert_element_type | solution.py:42
  402.2 56.6 %all_to_all.96 = bf16[1024,2,1024]{2,1,0:T(2,128)(2,1)S(1)} all-to-all(bf16[1024,2,1024]{2,1,0:T(2,128)(2,1)} %copy.138), channel_id=1, replica_groups=mesh['seq'=8,'head'=4] {'head'}, dimensions={0} | all-to-all | bytes 8388608 | tf_op jit(solution)/shard_map/all_to_all | solution.py:134
  458.7 3.3 copy.139
  462.1 6.2 %copy.140 = bf16[256,4,2,1024]{0,3,2,1:T(8,128)(2,1)} copy(bf16[256,4,2,1024]{3,0,1,2:T(8,128)(2,1)} %bitcast.162) | data formatting | bytes 8388608 | tf_op jit(solution)/shard_map/all_to_all | solution.py:134
  468.3 6.3 %copy.141 = bf16[256,8192]{1,0:T(8,128)(2,1)} copy(bf16[256,8192]{0,1:T(8,128)(2,1)} %bitcast.163) | data formatting | bytes 8388608 | tf_op jit(solution)/shard_map/reshape | solution.py:135
  (75 shorter events, 23.8 us)
Async XLA Ops:
  1.7 6.8 %all-to-all-start.3 = ((f32[256,8,16]{0,2,1:T(8,128)}), f32[256,8,16]{0,2,1:T(8,128)S(1)}, u32[]{:S(2)}, u32[]{:S(2)}) async-start(f32[256,8,16]{0,2,1:T(8,128)} %bitcast.22), calls=%async_computation.3 | async-start | bytes 262144 | tf_op jit(solution)/shard_map/all_to_all | solution.py:69
  8.5 7.9 %all-to-all-start.4 = ((f32[256,8,16]{0,2,1:T(8,128)}), f32[256,8,16]{0,2,1:T(8,128)S(1)}, u32[]{:S(2)}, u32[]{:S(2)}) async-start(f32[256,8,16]{0,2,1:T(8,128)} %bitcast.28), calls=%async_computation.4 | async-start | bytes 262144 | tf_op jit(solution)/shard_map/all_to_all | solution.py:68
  16.4 18.9 %all-to-all-start.1 = ((bf16[256,8,128]{2,0,1:T(8,128)(2,1)}), bf16[256,8,128]{2,0,1:T(8,128)(2,1)}, u32[]{:S(2)}, u32[]{:S(2)}) async-start(bf16[256,8,128]{2,0,1:T(8,128)(2,1)} %copy.121), calls=%async_computation.1 | async-start | bytes 1048576 | tf_op jit(solution)/shard_map/all_to_all | solution.py:65
  28.7 11.6 %copy-start = (bf16[256,8,128]{2,1,0:T(8,128)(2,1)S(1)}, bf16[256,8,128]{2,1,0:T(8,128)(2,1)}, u32[]{:S(2)}) copy-start(bf16[256,8,128]{2,1,0:T(8,128)(2,1)} %param.16) | copy-start | bytes 1572868
  35.3 12.3 %copy-start.2 = (f32[32]{0:T(128)S(1)}, f32[32]{0:T(128)}, u32[]{:S(2)}) copy-start(f32[32]{0:T(128)} %param.20) | copy-start | bytes 388
  35.3 51.4 %all-to-all-start = ((bf16[256,8,1024]{2,0,1:T(8,128)(2,1)}), bf16[256,8,1024]{2,0,1:T(8,128)(2,1)}, u32[]{:S(2)}, u32[]{:S(2)}) async-start(bf16[256,8,1024]{2,0,1:T(8,128)(2,1)} %copy.119), calls=%async_computation | async-start | bytes 8388608 | tf_op jit(solution)/shard_map/all_to_all | solution.py:62
  86.7 12.3 %all-to-all-start.2 = ((bf16[256,8,128]{2,0,1:T(8,128)(2,1)}), bf16[256,8,128]{2,0,1:T(8,128)(2,1)S(1)}, u32[]{:S(2)}, u32[]{:S(2)}) async-start(bf16[256,8,128]{2,0,1:T(8,128)(2,1)} %copy.122), calls=%async_computation.2 | async-start | bytes 1048576 | tf_op jit(solution)/shard_map/all_to_all | solution.py:64
  98.9 52.9 %all-to-all-start.5 = ((bf16[256,8,1024]{0,2,1:T(8,128)(2,1)}), bf16[256,8,1024]{0,2,1:T(8,128)(2,1)}, u32[]{:S(2)}, u32[]{:S(2)}) async-start(bf16[256,8,1024]{0,2,1:T(8,128)(2,1)} %bitcast.161), calls=%async_computation.5 | async-start | bytes 8388608 | tf_op jit(solution)/shard_map/all_to_all | solution.py:63
  158.3 25.8 %collective-permute-start = (f32[2,16,64,128]{3,2,1,0:T(8,128)S(1)}, f32[2,16,64,128]{3,2,1,0:T(8,128)S(1)}, u32[]{:S(2)}, u32[]{:S(2)}) collective-permute-start(f32[2,16,64,128]{3,2,1,0:T(8,128)S(1)} %multiply_add_fusion.2), channel_id=1, source_target_pairs={{0,4},{4,8},{8,12},{12,16},{16,20},{20,24},{24,28},{1,5},{5,9},{9,... | collective-permute-start | bytes 3145736 | tf_op jit(solution)/shard_map/while/body/eval_jaxpr/ppermute | solution.py:12
  184.2 25.0 %collective-permute-start = (f32[2,16,64,128]{3,2,1,0:T(8,128)S(1)}, f32[2,16,64,128]{3,2,1,0:T(8,128)S(1)}, u32[]{:S(2)}, u32[]{:S(2)}) collective-permute-start(f32[2,16,64,128]{3,2,1,0:T(8,128)S(1)} %multiply_add_fusion.2), channel_id=1, source_target_pairs={{0,4},{4,8},{8,12},{12,16},{16,20},{20,24},{24,28},{1,5},{5,9},{9,... | collective-permute-start | bytes 3145736 | tf_op jit(solution)/shard_map/while/body/eval_jaxpr/ppermute | solution.py:12
  209.4 25.0 %collective-permute-start = (f32[2,16,64,128]{3,2,1,0:T(8,128)S(1)}, f32[2,16,64,128]{3,2,1,0:T(8,128)S(1)}, u32[]{:S(2)}, u32[]{:S(2)}) collective-permute-start(f32[2,16,64,128]{3,2,1,0:T(8,128)S(1)} %multiply_add_fusion.2), channel_id=1, source_target_pairs={{0,4},{4,8},{8,12},{12,16},{16,20},{20,24},{24,28},{1,5},{5,9},{9,... | collective-permute-start | bytes 3145736 | tf_op jit(solution)/shard_map/while/body/eval_jaxpr/ppermute | solution.py:12
  234.5 24.2 %collective-permute-start = (f32[2,16,64,128]{3,2,1,0:T(8,128)S(1)}, f32[2,16,64,128]{3,2,1,0:T(8,128)S(1)}, u32[]{:S(2)}, u32[]{:S(2)}) collective-permute-start(f32[2,16,64,128]{3,2,1,0:T(8,128)S(1)} %multiply_add_fusion.2), channel_id=1, source_target_pairs={{0,4},{4,8},{8,12},{12,16},{16,20},{20,24},{24,28},{1,5},{5,9},{9,... | collective-permute-start | bytes 3145736 | tf_op jit(solution)/shard_map/while/body/eval_jaxpr/ppermute | solution.py:12
  258.9 23.3 %collective-permute-start = (f32[2,16,64,128]{3,2,1,0:T(8,128)S(1)}, f32[2,16,64,128]{3,2,1,0:T(8,128)S(1)}, u32[]{:S(2)}, u32[]{:S(2)}) collective-permute-start(f32[2,16,64,128]{3,2,1,0:T(8,128)S(1)} %multiply_add_fusion.2), channel_id=1, source_target_pairs={{0,4},{4,8},{8,12},{12,16},{16,20},{20,24},{24,28},{1,5},{5,9},{9,... | collective-permute-start | bytes 3145736 | tf_op jit(solution)/shard_map/while/body/eval_jaxpr/ppermute | solution.py:12
  282.3 22.4 %collective-permute-start = (f32[2,16,64,128]{3,2,1,0:T(8,128)S(1)}, f32[2,16,64,128]{3,2,1,0:T(8,128)S(1)}, u32[]{:S(2)}, u32[]{:S(2)}) collective-permute-start(f32[2,16,64,128]{3,2,1,0:T(8,128)S(1)} %multiply_add_fusion.2), channel_id=1, source_target_pairs={{0,4},{4,8},{8,12},{12,16},{16,20},{20,24},{24,28},{1,5},{5,9},{9,... | collective-permute-start | bytes 3145736 | tf_op jit(solution)/shard_map/while/body/eval_jaxpr/ppermute | solution.py:12
  304.9 21.6 %collective-permute-start = (f32[2,16,64,128]{3,2,1,0:T(8,128)S(1)}, f32[2,16,64,128]{3,2,1,0:T(8,128)S(1)}, u32[]{:S(2)}, u32[]{:S(2)}) collective-permute-start(f32[2,16,64,128]{3,2,1,0:T(8,128)S(1)} %multiply_add_fusion.2), channel_id=1, source_target_pairs={{0,4},{4,8},{8,12},{12,16},{16,20},{20,24},{24,28},{1,5},{5,9},{9,... | collective-permute-start | bytes 3145736 | tf_op jit(solution)/shard_map/while/body/eval_jaxpr/ppermute | solution.py:12
  373.6 8.7 %copy-start.1 = (f32[2,1024]{1,0:T(2,128)S(1)}, f32[2,1024]{1,0:T(2,128)}, u32[]{:S(2)}) copy-start(f32[2,1024]{1,0:T(2,128)} %mul.139) | copy-start | bytes 24580
where the time goes:
time: 481 us; the launch traced here: 475 us
  waiting for transfers between devices  198 us (41%)
  local copies, waits for them, and re-layouts  106 us (22%)
  blocking collectives  56.6 us (12%)
  matrix products  41.3 us (9%)
  starting transfers between devices  41.2 us (9%)
  other arithmetic  31.6 us (7%)
    ppermute x7, waiting for transfers between devices, passed_along(): lax.ppermute(value, axis, [(source, source + steps) for source in range(l...  158 us
    all_to_all x1, blocking collectives, shards(): lax.all_to_all(mixed_here, 'head', split_axis=0, concat_axis=1, tiled=True)  56.6 us
    all_to_all x1, waiting for transfers between devices, shards(): lax.all_to_all(feature_groups, 'head', split_axis=1, concat_axis=0, tiled...  32.7 us
    convert_element_type x2, local copies, waits for them, and re-layouts, normalize(): values.astype(jnp.float32) * jax.nn.silu(gate_part.astype(jnp.float32))  24.5 us
    unnamed x12, local copies, waits for them, and re-layouts  18.8 us
    convert_element_type x2, local copies, waits for them, and re-layouts, normalize(): gate_part.astype(jnp.float32)  17.5 us
    dot_general x2, matrix products, block_terms(): jnp.einsum('ghts,sghp->tghp', weights, feature_block, preferred_element_t...  14.7 us
    dot_general x1, matrix products, shards(): jnp.einsum('ktgn,kghpn->ktghp', c_blocks.astype(jnp.float32), states, pre...  13.8 us
  transfers between devices with their start and end apart: 13, of which 12 were waited for; matrix products, arithmetic and copies ran while one was open for 16% of the time, Pallas kernels for 0%

commit v1 on v0

v1 whole, which is shorter than its diff:
```python
import jax
import jax.numpy as jnp
from jax import lax
from jax.experimental import pallas as pl
from jax.experimental.pallas import tpu as pltpu
from jax.sharding import PartitionSpec as P

SUB = 128
MID = SUB // 2 - 1
EXTRA = 16
PLANE = 4
AXES = ("seq", "head")
F32, BF16 = jnp.float32, jnp.bfloat16
VM = pl.BlockSpec(memory_space=pltpu.VMEM)
SM = pl.BlockSpec(memory_space=pltpu.SMEM)


def split_two(value):
    high = value.astype(BF16)
    return high, (value - high.astype(F32)).astype(BF16)


def dot(a, b):
    return lax.dot_general(a, b, (((1,), (0,)), ((), ())), preferred_element_type=F32)


def dot_tn(a, b):
    return lax.dot_general(a, b, (((0,), (0,)), ((), ())), preferred_element_type=F32)


def dot_nt(a, b):
    return lax.dot_general(a, b, (((1,), (1,)), ((), ())), preferred_element_type=F32)


def spread_matrix(group, heads, per_group, width):
    row = lax.broadcasted_iota(jnp.int32, (2 * heads, width), 0)
    column = lax.broadcasted_iota(jnp.int32, (2 * heads, width), 1)
    head = group * per_group + column // (width // per_group)
    return ((row == head) | (row == head + heads)).astype(BF16)


def pair_row(later, earlier, subs):
    return 1 + 2 * subs + later * (later - 1) // 2 + earlier


def decay_of(ref):
    rows = ref[-EXTRA:, :].astype(F32)
    return rows[0:1] + rows[1:2]


def put_decay(ref, decay):
    high, low = split_two(decay)
    row = lax.broadcasted_iota(jnp.int32, (EXTRA, decay.shape[1]), 0)
    both = jnp.where(row == 0, high.astype(F32), jnp.where(row == 1, low.astype(F32), 0.0))
    ref[-EXTRA:, :] = both.astype(BF16)


def write_scales(decay_ref, step_ref, sx_ref, sr_ref):
    rows, heads = decay_ref.shape
    subs = rows // SUB
    decay = decay_ref[...]
    high = decay.astype(BF16)
    rest = decay - high.astype(F32)
    mid = rest.astype(BF16)
    low = (rest - mid.astype(F32)).astype(BF16)
    row = lax.broadcasted_iota(jnp.int32, (rows, rows), 0)
    column = lax.broadcasted_iota(jnp.int32, (rows, rows), 1)
    lower = (row >= column).astype(BF16)
    cum = dot(lower, high) + dot(lower, mid) + dot(lower, low)
    centre = [cum[b * SUB + MID : b * SUB + MID + 1] for b in range(subs)]
    last = cum[rows - 1 : rows]
    for b in range(subs):
        part = slice(b * SUB, (b + 1) * SUB)
        off = cum[part] - centre[b]
        high, low = split_two(jnp.exp(-off) * step_ref[part, :])
        sx_ref[part, :heads] = high
        sx_ref[part, heads:] = low
        high, low = split_two(jnp.exp(off))
        sr_ref[part, :heads] = high
        sr_ref[part, heads:] = low
    scalars = [last] + [last - c for c in centre] + centre
    for b in range(subs):
        scalars += [centre[b] - centre[a] for a in range(b)]
    pad = jnp.zeros((EXTRA - len(scalars), heads), F32)
    high, low = split_two(jnp.exp(jnp.concatenate(scalars + [pad], axis=0)))
    sx_ref[rows:, :heads] = high
    sx_ref[rows:, heads:] = low


def scaled_features(x_ref, sx_ref, spread):
    rows = x_ref.shape[0]
    scale = dot(sx_ref[...], spread)
    return (x_ref[...].astype(F32) * scale[:rows]).astype(BF16), scale[rows:]


def update_of(xa, b_group, scalars, out_ref):
    rows = xa.shape[0]
    total = None
    for b in range(rows // SUB):
        part = slice(b * SUB, (b + 1) * SUB)
        term = dot_tn(b_group[part], xa[part]) * scalars[1 + b : 2 + b]
        total = term if total is None else total + term
    out_ref[:-EXTRA, :] = total.astype(BF16)
    put_decay(out_ref, scalars[0:1])


def first_kernel(ids, x_ref, b_ref, step_ref, decay_ref, u_ref, bg_ref, sx_ref, sr_ref, b32):
    i = pl.program_id(0)
    rows, groups, state = b_ref.shape
    heads = step_ref.shape[1]
    per_group = heads // groups

    @pl.when(i == 0)
    def _():
        write_scales(decay_ref, step_ref, sx_ref, sr_ref)
        b32[...] = b_ref[...].astype(F32).reshape(rows * groups, state)
        for g in range(groups):
            bg_ref[g] = b32[pl.ds(g, rows, stride=groups), :].astype(BF16)

    group = ids[0] + i
    spread = spread_matrix(group, heads, per_group, x_ref.shape[1])
    xa, scalars = scaled_features(x_ref, sx_ref, spread)
    update_of(xa, bg_ref[group], scalars, u_ref.at[0])


def second_kernel(ids, x_ref, bg_ref, sx_ref, u_ref):
    groups = bg_ref.shape[0]
    heads = sx_ref.shape[1] // 2
    group = ids[1] + pl.program_id(0)
    spread = spread_matrix(group, heads, heads // groups, x_ref.shape[1])
    xa, scalars = scaled_features(x_ref, sx_ref, spread)
    update_of(xa, bg_ref[group], scalars, u_ref.at[0])


def local_kernel(x_ref, c_ref, bg_ref, sx_ref, sr_ref, skip_ref, y_ref, cg_ref, c32):
    group = pl.program_id(0)
    rows, groups, state = c_ref.shape
    heads = sx_ref.shape[1] // 2
    subs = rows // SUB

    @pl.when(group == 0)
    def _():
        c32[...] = c_ref[...].astype(F32).reshape(rows * groups, state)
        for g in range(groups):
            cg_ref[g] = c32[pl.ds(g, rows, stride=groups), :].astype(BF16)

    spread = spread_matrix(group, heads, heads // groups, x_ref.shape[1])
    xa, scalars = scaled_features(x_ref, sx_ref, spread)
    row_scale = dot(sr_ref[...], spread)
    high, low = split_two(jnp.broadcast_to(skip_ref[...], (EXTRA, heads)))
    skip = dot(jnp.concatenate([high, low], axis=1), spread)[0:1]
    row = lax.broadcasted_iota(jnp.int32, (SUB, SUB), 0)
    column = lax.broadcasted_iota(jnp.int32, (SUB, SUB), 1)
    b_group, c_group = bg_ref[group], cg_ref[group]
    for b in range(subs):
        part = slice(b * SUB, (b + 1) * SUB)
        scores = jnp.where(row >= column, dot_nt(c_group[part], b_group[part]), 0.0)
        inner = dot(scores.astype(BF16), xa[part])
        for a in range(b):
            other = slice(a * SUB, (a + 1) * SUB)
            scores = dot_nt(c_group[part], b_group[other]).astype(BF16)
            at = pair_row(b, a, subs)
            inner = inner + dot(scores, xa[other]) * scalars[at : at + 1]
        y_ref[part, :] = row_scale[part] * inner + skip * x_ref[part, :].astype(F32)


def pair_down_kernel(ids, own_ref, far_ref, *outs):
    core, chip = ids[2], ids[3]

    def run(first, second):
        for m in range(PLANE):
            slot = chip ^ m
            d0, d1 = decay_of(first.at[slot]), decay_of(second.at[slot])
            u0, u1 = first[slot, :-EXTRA, :], second[slot, :-EXTRA, :]
            outs[m][:-EXTRA, :] = (d1 * u0.astype(F32) + u1.astype(F32)).astype(BF16)
            put_decay(outs[m], d0 * d1)

    pl.when(core == 0)(lambda: run(own_ref, far_ref))
    pl.when(core == 1)(lambda: run(far_ref, own_ref))


def plane_down_kernel(ids, p0, p1, p2, p3, near_ref, away_ref, held):
    chip, side = ids[3], ids[4]
    for m, piece in enumerate((p0, p1, p2, p3)):
        held[chip ^ m] = piece[...]
    total, decay = held[0, :-EXTRA, :].astype(F32), decay_of(held.at[0])
    for k in range(1, PLANE):
        d = decay_of(held.at[k])
        total = d * total + held[k, :-EXTRA, :].astype(F32)
        decay = d * decay
    half = total.shape[1] // 2

    def put(low_ref, high_ref):
        low_ref[:-EXTRA, :] = total[:, :half].astype(BF16)
        high_ref[:-EXTRA, :] = total[:, half:].astype(BF16)
        put_decay(low_ref, decay[:, :half])
        put_decay(high_ref, decay[:, half:])

    pl.when(side == 0)(lambda: put(near_ref, away_ref))
    pl.when(side == 1)(lambda: put(away_ref, near_ref))


def side_down_kernel(ids, own_ref, far_ref, out_ref):
    def run(first, second):
        d0, d1 = decay_of(first), decay_of(second)
        out_ref[:-EXTRA, :] = (
            d1 * first[:-EXTRA, :].astype(F32) + second[:-EXTRA, :].astype(F32)
        ).astype(BF16)
        put_decay(out_ref, d0 * d1)

    pl.when(ids[4] == 0)(lambda: run(own_ref, far_ref))
    pl.when(ids[4] == 1)(lambda: run(far_ref, own_ref))


def side_up_kernel(ids, enter_ref, own_ref, far_ref, near_ref, away_ref):
    enter = enter_ref[:-EXTRA, :]

    def run(first, first_out, second_out):
        first_out[...] = enter
        after = decay_of(first) * enter.astype(F32) + first[:-EXTRA, :].astype(F32)
        second_out[...] = after.astype(BF16)

    pl.when(ids[4] == 0)(lambda: run(own_ref, near_ref, away_ref))
    pl.when(ids[4] == 1)(lambda: run(far_ref, away_ref, near_ref))


def plane_up_kernel(ids, near_ref, away_ref, p0, p1, p2, p3, o0, o1, o2, o3, held, state):
    chip, side = ids[3], ids[4]
    half = near_ref.shape[1]
    for m, piece in enumerate((p0, p1, p2, p3)):
        held[chip ^ m] = piece[...]

    def enter(low_ref, high_ref):
        state[0, :, :half] = low_ref[...]
        state[0, :, half:] = high_ref[...]

    pl.when(side == 0)(lambda: enter(near_ref, away_ref))
    pl.when(side == 1)(lambda: enter(away_ref, near_ref))
    now = state[0].astype(F32)
    for k in range(1, PLANE):
        now = decay_of(held.at[k - 1]) * now + held[k - 1, :-EXTRA, :].astype(F32)
        state[k] = now.astype(BF16)
    for m, out in enumerate((o0, o1, o2, o3)):
        out[...] = state[chip ^ m]


def pair_up_kernel(ids, own_ref, far_ref, s0, s1, s2, s3, mine_ref, send_ref):
    core, chip = ids[2], ids[3]

    def run(first, first_out, second_out):
        for m, piece in enumerate((s0, s1, s2, s3)):
            slot = chip ^ m
            first_out[slot] = piece[...]
            after = decay_of(first.at[slot]) * piece[...].astype(F32)
            second_out[slot] = (after + first[slot, :-EXTRA, :].astype(F32)).astype(BF16)

    pl.when(core == 0)(lambda: run(own_ref, mine_ref, send_ref))
    pl.when(core == 1)(lambda: run(far_ref, send_ref, mine_ref))


def small_call(kernel, ids, args, outs, scratch=()):
    size = sum(a.size * 2 for a in args) + sum(2 * o.size for o in outs)
    return pl.pallas_call(
        kernel,
        out_shape=outs,
        in_specs=[SM] + [VM] * len(args),
        out_specs=[VM] * len(outs),
        scratch_shapes=list(scratch),
        cost_estimate=pl.CostEstimate(flops=size, bytes_accessed=size, transcendentals=0),
    )(ids, *args)


def exchange(value, mask, count):
    return lax.ppermute(value, AXES, [(i, i ^ mask) for i in range(count)])


def shifted(value, steps, count):
    return lax.ppermute(value, AXES, [(i, i + steps) for i in range(count - steps)])


def scan_groups(total, stride, count):
    places = count // stride

    def parts(message):
        decay = message[-EXTRA].astype(F32) + message[-EXTRA + 1].astype(F32)
        return message[:-EXTRA].astype(F32), decay

    def packed(value, decay):
        high, low = split_two(decay)
        rest = jnp.zeros((EXTRA - 2, decay.shape[0]), BF16)
        return jnp.concatenate([value.astype(BF16), high[None], low[None], rest], axis=0)

    covered = shifted(total, stride, count)
    reach = 1
    while reach < places - 1:
        value, decay = parts(covered)
        own, own_decay = parts(total)
        longer = packed(own_decay[None] * value + own, own_decay * decay)
        far, far_decay = parts(shifted(longer, stride * (reach + 1), count))
        covered = packed(decay[None] * far + value, decay * far_decay)
        reach = 2 * reach + 1
    return covered


def finish(group, y_ref, cg_ref, sx_ref, sr_ref, s_ref, gate_ref, gain_ref, out_ref):
    rows, width = y_ref.shape
    groups = cg_ref.shape[0]
    heads = sx_ref.shape[1] // 2
    subs = rows // SUB
    spread = spread_matrix(group, heads, heads // groups, width)
    row_scale = dot(sr_ref[...], spread)
    scalars = dot(sx_ref[rows:, :], spread)
    c_group, state = cg_ref[group], s_ref[0]
    for b in range(subs):
        part = slice(b * SUB, (b + 1) * SUB)
        at = 1 + subs + b
        carried = dot(c_group[part], state) * scalars[at : at + 1]
        ssm = (y_ref[part, :] + row_scale[part] * carried).astype(BF16).astype(F32)
        gate = gate_ref[part, :].astype(F32)
        gated = ssm * (gate / (1.0 + jnp.exp(-gate)))
        mean = jnp.mean(gated * gated, axis=1, keepdims=True)
        out_ref[part, :] = (gated * lax.rsqrt(mean + 1e-05) * gain_ref[...]).astype(BF16)


def own_finish_kernel(ids, *refs):
    finish(ids[1] + pl.program_id(0), *refs)


def far_finish_kernel(ids, *refs):
    finish(ids[0] + pl.program_id(0), *refs[:-2], refs[-1])


def shards(features, gate_input, bmat, cmat, step_size, log_decay, skip, norm_gain):
    rows, inner = features.shape
    groups, state = bmat.shape[1:]
    heads = step_size.shape[1]
    width = inner // groups
    half = groups // 2
    count = lax.axis_size("seq") * lax.axis_size("head")
    me = lax.axis_index("seq") * lax.axis_size("head") + lax.axis_index("head")
    core = me & 1
    chip = (me >> 1) & (PLANE - 1)
    side = (me >> 3) & 1
    ids = jnp.stack([(1 - core) * half, core * half, core, chip, side]).astype(jnp.int32)
    tall = state + EXTRA

    def out(*shape, kind=BF16):
        return jax.ShapeDtypeStruct(shape, kind)

    def whole(*shape):
        return pl.BlockSpec(shape, lambda i, *_: (0,) * len(shape))

    def cols(which):
        return pl.BlockSpec((rows, width), lambda i, ids: (0, ids[which] + i))

    slot_spec = pl.BlockSpec((1, tall, width), lambda i, *_: (i, 0, 0))
    grid = pltpu.PrefetchScalarGridSpec
    small = whole(rows + EXTRA, 2 * heads)
    away, bg, sx, sr = pl.pallas_call(
        first_kernel,
        grid_spec=grid(
            num_scalar_prefetch=1,
            grid=(half,),
            in_specs=[cols(0), whole(rows, groups, state), whole(rows, heads), whole(rows, heads)],
            out_specs=[slot_spec, whole(groups, rows, state), small, whole(rows, 2 * heads)],
            scratch_shapes=[pltpu.VMEM((rows * groups, state), F32)],
        ),
        out_shape=[
            out(half, tall, width),
            out(groups, rows, state),
            out(rows + EXTRA, 2 * heads),
            out(rows, 2 * heads),
        ],
        cost_estimate=pl.CostEstimate(flops=10**9, bytes_accessed=8 * 2**20, transcendentals=0),
    )(ids, features, bmat, step_size, log_decay)
    pair_far = exchange(away, 1, count)
    (pair_own,) = pl.pallas_call(
        second_kernel,
        grid_spec=grid(
            num_scalar_prefetch=1,
            grid=(half,),
            in_specs=[cols(1), whole(groups, rows, state), small],
            out_specs=[slot_spec],
        ),
        out_shape=[out(half, tall, width)],
        cost_estimate=pl.CostEstimate(flops=10**9, bytes_accessed=8 * 2**20, transcendentals=0),
    )(ids, features, bg, sx)

    pieces = small_call(pair_down_kernel, ids, (pair_own, pair_far), [out(tall, width)] * PLANE)
    pieces = [pieces[0]] + [exchange(pieces[m], 2 * m, count) for m in range(1, PLANE)]

    skips = skip
    for bit in range((heads // skip.shape[0]).bit_length() - 1):
        other = exchange(skips, 1 << bit, count)
        first = (lax.axis_index("head") >> bit) & 1 == 0
        skips = jnp.where(first, jnp.concatenate([skips, other]), jnp.concatenate([other, skips]))
    local, cg = pl.pallas_call(
        local_kernel,
        grid=(groups,),
        in_specs=[
            pl.BlockSpec((rows, width), lambda i: (0, i)),
            whole(rows, groups, state),
            whole(groups, rows, state),
            small,
            whole(rows, 2 * heads),
            whole(1, heads),
        ],
        out_specs=[pl.BlockSpec((rows, width), lambda i: (0, i)), whole(groups, rows, state)],
        out_shape=[out(rows, inner, kind=F32), out(groups, rows, state)],
        scratch_shapes=[pltpu.VMEM((rows * groups, state), F32)],
        cost_estimate=pl.CostEstimate(flops=10**10, bytes_accessed=16 * 2**20, transcendentals=0),
    )(features, cmat, bg, sx, sr, skips.reshape(1, heads))

    side_own, side_send = small_call(
        plane_down_kernel,
        ids,
        pieces,
        [out(tall, width // 2)] * 2,
        [pltpu.VMEM((PLANE, tall, width), BF16)],
    )
    side_far = exchange(side_send, 8, count)
    (total,) = small_call(side_down_kernel, ids, (side_own, side_far), [out(tall, width // 2)])
    enter = scan_groups(total, 16, count)
    near, send = small_call(
        side_up_kernel, ids, (enter, side_own, side_far), [out(state, width // 2)] * 2
    )
    far = exchange(send, 8, count)
    states = small_call(
        plane_up_kernel,
        ids,
        (near, far, *pieces),
        [out(state, width)] * PLANE,
        [pltpu.VMEM((PLANE, tall, width), BF16), pltpu.VMEM((PLANE, state, width), BF16)],
    )
    states = [states[0]] + [exchange(states[m], 2 * m, count) for m in range(1, PLANE)]
    mine, send = small_call(
        pair_up_kernel, ids, (pair_own, pair_far, *states), [out(half, state, width)] * 2
    )
    theirs = exchange(send, 1, count)

    def finish_specs(which):
        return [
            cols(which),
            whole(groups, rows, state),
            small,
            whole(rows, 2 * heads),
            pl.BlockSpec((1, state, width), lambda i, ids: (i, 0, 0)),
            cols(which),
            pl.BlockSpec((1, width), lambda i, ids: (0, ids[which] + i)),
        ]

    gain = norm_gain.reshape(1, inner)
    cost = pl.CostEstimate(flops=10**9, bytes_accessed=10 * 2**20, transcendentals=0)
    (result,) = pl.pallas_call(
        own_finish_kernel,
        grid_spec=grid(
            num_scalar_prefetch=1, grid=(half,), in_specs=finish_specs(1), out_specs=[cols(1)]
        ),
        out_shape=[out(rows, inner)],
        cost_estimate=cost,
    )(ids, local, cg, sx, sr, mine, gate_input, gain)
    (result,) = pl.pallas_call(
        far_finish_kernel,
        grid_spec=grid(
            num_scalar_prefetch=1,
            grid=(half,),
            in_specs=finish_specs(0) + [pl.BlockSpec(memory_space=pl.ANY)],
            out_specs=[cols(0)],
        ),
        out_shape=[out(rows, inner)],
        input_output_aliases={8: 0},
        cost_estimate=cost,
    )(ids, local, cg, sx, sr, theirs, gate_input, gain, result)
    return result


def solution(mesh):
    return jax.shard_map(
        shards,
        mesh=mesh,
        in_specs=(
            P(("seq", "head"), None),
            P(("seq", "head"), None),
            P(("seq", "head"), None, None),
            P(("seq", "head"), None, None),
            P(("seq", "head"), None),
            P(("seq", "head"), None),
            P("head"),
            P(),
        ),
        out_specs=P(("seq", "head"), None),
        check_vma=False,
    )
```

time: 481 us -> 116 us (0.24); the launches traced: 475 us -> 115 us
  waiting for transfers between devices: 198 us -> 35.7 us
  local copies, waits for them, and re-layouts: 106 us -> 6.08 us
  Pallas kernels: 0 us -> 57.3 us
  blocking collectives: 56.6 us -> 0 us
  matrix products: 41.3 us -> 0 us
  other arithmetic: 31.6 us -> 0.66 us
  starting transfers between devices: 41.2 us -> 15.5 us
    ppermute x7 -> x13, waiting for transfers between devices: 158 us -> 35.7 us  [the longest x12 26.3 us: exchange(): return lax.ppermute(value, AXES, [(i, i ^ mask) for i in range(count)])]
    pallas_call x0 -> x11, Pallas kernels: none -> 57.3 us  [the longest x6 15.5 us: small_call(): pl.pallas_call(kernel, out_shape=outs, in_specs=[SM] + [VM] * len(args),...]
    all_to_all x1 -> x0, blocking collectives: 56.6 us -> none  [shards(): lax.all_to_all(mixed_here, 'head', split_axis=0, concat_axis=1, tiled=True)]
    convert_element_type x5 -> x0, local copies, waits for them, and re-layouts: 53.2 us -> none  [the longest x2 24.5 us: normalize(): values.astype(jnp.float32) * jax.nn.silu(gate_part.astype(jnp.float32))]
    dot_general x7 -> x0, matrix products: 41.3 us -> none  [the longest x2 14.7 us: block_terms(): jnp.einsum('ghts,sghp->tghp', weights, feature_block, preferred_element_t...]
    all_to_all x6 -> x0, waiting for transfers between devices: 39.8 us -> none  [the longest x1 32.7 us: shards(): lax.all_to_all(feature_groups, 'head', split_axis=1, concat_axis=0, tiled...]
    all_to_all x6 -> x0, starting transfers between devices: 32.1 us -> none  [the longest x1 6.66 us: shards(): lax.all_to_all(gate_groups, 'head', split_axis=1, concat_axis=0, tiled=True)]
    all_to_all x3 -> x0, local copies, waits for them, and re-layouts: 15.8 us -> none  [the longest x2 9.56 us: shards(): lax.all_to_all(mixed_here, 'head', split_axis=0, concat_axis=1, tiled=True)]
  transfers between devices with their start and end apart: 13 -> 13, of which waited for: 12 -> 7; matrix products, arithmetic and copies ran while one was open for 16% -> 1% of each run, Pallas kernels for 0% -> 27%
where the time goes in v1:
time: 116 us; the launch traced here: 115 us
  Pallas kernels  57.3 us (49%)
  waiting for transfers between devices  35.7 us (31%)
  starting transfers between devices  15.5 us (13%)
  local copies, waits for them, and re-layouts  6.08 us (5%)
    ppermute x12, waiting for transfers between devices, exchange(): return lax.ppermute(value, AXES, [(i, i ^ mask) for i in range(count)])  26.3 us
    pallas_call x6, Pallas kernels, small_call(): pl.pallas_call(kernel, out_shape=outs, in_specs=[SM] + [VM] * len(args),...  15.5 us
    ppermute x12, starting transfers between devices, exchange(): return lax.ppermute(value, AXES, [(i, i ^ mask) for i in range(count)])  14.3 us
    pallas_call x1, Pallas kernels, shards(): pl.pallas_call(local_kernel, grid=(groups,), in_specs=[pl.BlockSpec((rows...  12.8 us
    ppermute x1, waiting for transfers between devices, shifted(): lax.ppermute(value, AXES, [(i, i + steps) for i in range(count - steps)])  9.38 us
    pallas_call x1, Pallas kernels, shards(): pl.pallas_call(far_finish_kernel, grid_spec=grid(num_scalar_prefetch=1, g...  8.41 us
    pallas_call x1, Pallas kernels, shards(): pl.pallas_call(own_finish_kernel, grid_spec=grid(num_scalar_prefetch=1, g...  8.41 us
    pallas_call x1, Pallas kernels, shards(): pl.pallas_call(first_kernel, grid_spec=grid(num_scalar_prefetch=1, grid=(...  6.37 us
  transfers between devices with their start and end apart: 13, of which 7 were waited for; matrix products, arithmetic and copies ran while one was open for 1% of the time, Pallas kernels for 27%

profile of v1, /device:TPU:31, one launch (start us, length us, event | category | flops | bytes accessed | tf_op | source)
XLA Modules:
  0.0 115.3 jit_solution(6142189397296859234)
XLA Ops:
  0.0 0.7 stack.23.ids
  0.7 6.4 %shard_map.82 = (bf16[4,144,1024]{2,1,0:T(8,128)(2,1)}, bf16[8,256,128]{2,1,0:T(8,128)(2,1)}, bf16[272,256]{1,0:T(8,128)(2,1)}, bf16[256,256]{1,0:T(8,128)(2,1)}) custom-call(s32[5]{0:T(128)} %stack.23.ids, bf16[256,8192]{1,0:T(8,128)(2,1)} %x_ref.5, bf16[256,8,128]{2,1,0:T(8,128)(2,1)} %b_ref.1, f32[256,128]{1,0:T(8,128)} %step_ref.1, f32[256,128]{1,0:T(8,128)} %decay_ref.1), custom_call_target="tpu_custom_call" | custom-call | flops 1000000000 | bytes 8388608 | tf_op jit(solution)/shard_map/pallas_call | solution.py:359
  7.0 0.7 collective-permute-start.2
  7.7 5.8 %shard_map.84.own_ref = bf16[4,144,1024]{2,1,0:T(8,128)(2,1)} custom-call(s32[5]{0:T(128)} %stack.23.ids, bf16[256,8192]{1,0:T(8,128)(2,1)} %x_ref.5, bf16[8,256,128]{2,1,0:T(8,128)(2,1)} %get-tuple-element.25.bg_ref, bf16[272,256]{1,0:T(8,128)(2,1)} %get-tuple-element.26.sx_ref.refs_2_), custom_call_target="tpu_custom_call" | custom-call | flops 1000000000 | bytes 8388608 | tf_op jit(solution)/shard_map/pallas_call | solution.py:377
  13.5 0.0 collective-permute-done.2.far_ref
  13.5 1.0 copy-done
  14.5 3.0 %shard_map.85 = (bf16[144,1024]{1,0:T(8,128)(2,1)}, bf16[144,1024]{1,0:T(8,128)(2,1)}, bf16[144,1024]{1,0:T(8,128)(2,1)}, bf16[144,1024]{1,0:T(8,128)(2,1)}) custom-call(s32[5]{0:T(128)} %stack.23.ids, bf16[4,144,1024]{2,1,0:T(8,128)(2,1)} %shard_map.84.own_ref, bf16[4,144,1024]{2,1,0:T(8,128)(2,1)} %copy-done), custom_call_target="tpu_custom_call" | custom-call | flops 3538944 | bytes 3538944 | tf_op jit(solution)/shard_map/pallas_call | solution.py:263
  17.6 0.2 collective-permute-start.3
  17.8 0.3 collective-permute-start.4
  18.0 2.2 %collective-permute-start.5 = (bf16[144,1024]{1,0:T(8,128)(2,1)}, bf16[144,1024]{1,0:T(8,128)(2,1)S(1)}, u32[]{:S(2)}, u32[]{:S(2)}) collective-permute-start(bf16[144,1024]{1,0:T(8,128)(2,1)} %get-tuple-element.34), channel_id=1, source_target_pairs={{0,6},{1,7},{2,4},{3,5},{4,2},{5,3},{6,0},{7,1},{8,14},{9,15},{10,... | collective-permute-start | bytes 884744 | tf_op jit(solution)/shard_map/ppermute | solution.py:274
  20.2 6.1 %collective-permute-done.3.p1 = bf16[144,1024]{1,0:T(8,128)(2,1)S(1)} collective-permute-done((bf16[144,1024]{1,0:T(8,128)(2,1)}, bf16[144,1024]{1,0:T(8,128)(2,1)S(1)}, u32[]{:S(2)}, u32[]{:S(2)}) %collective-permute-start.3) | collective-permute-done | bytes 294944 | tf_op jit(solution)/shard_map/ppermute | solution.py:274
  26.3 0.0 collective-permute-done.4.p2
  26.3 7.2 %collective-permute-done.5.p3 = bf16[144,1024]{1,0:T(8,128)(2,1)S(1)} collective-permute-done((bf16[144,1024]{1,0:T(8,128)(2,1)}, bf16[144,1024]{1,0:T(8,128)(2,1)S(1)}, u32[]{:S(2)}, u32[]{:S(2)}) %collective-permute-start.5) | collective-permute-done | bytes 294944 | tf_op jit(solution)/shard_map/ppermute | solution.py:274
  33.6 0.7 copy-done.3
  34.3 2.4 %shard_map.86 = (bf16[144,512]{1,0:T(8,128)(2,1)}, bf16[144,512]{1,0:T(8,128)(2,1)}) custom-call(s32[5]{0:T(128)} %stack.23.ids, bf16[144,1024]{1,0:T(8,128)(2,1)} %get-tuple-element.31.p0, bf16[144,1024]{1,0:T(8,128)(2,1)} %copy-done.1, bf16[144,1024]{1,0:T(8,128)(2,1)} %copy-done.2, bf16[144,1024]{1,0:T(8,128)(2,1)} %copy-done.3), custom_call_target="tpu_custom_call" | custom-call | flops 1474560 | bytes 1474560 | tf_op jit(solution)/shard_map/pallas_call | solution.py:263
  36.7 0.2 collective-permute-start.6
  36.9 4.0 %collective-permute-done.6.far_ref = bf16[144,512]{1,0:T(8,128)(2,1)S(1)} collective-permute-done((bf16[144,512]{1,0:T(8,128)(2,1)}, bf16[144,512]{1,0:T(8,128)(2,1)S(1)}, u32[]{:S(2)}, u32[]{:S(2)}) %collective-permute-start.6) | collective-permute-done | bytes 147488 | tf_op jit(solution)/shard_map/ppermute | solution.py:274
  40.9 0.7 copy-done.5
  41.6 1.7 %shard_map.87 = bf16[144,512]{1,0:T(8,128)(2,1)} custom-call(s32[5]{0:T(128)} %stack.23.ids, bf16[144,512]{1,0:T(8,128)(2,1)} %get-tuple-element.35.own_ref, bf16[144,512]{1,0:T(8,128)(2,1)} %copy-done.5), custom_call_target="tpu_custom_call" | custom-call | flops 442368 | bytes 442368 | tf_op jit(solution)/shard_map/pallas_call | solution.py:263
  43.3 1.3 %collective-permute-start.7 = (bf16[144,512]{1,0:T(8,128)(2,1)}, bf16[144,512]{1,0:T(8,128)(2,1)S(1)}, u32[]{:S(2)}, u32[]{:S(2)}) collective-permute-start(bf16[144,512]{1,0:T(8,128)(2,1)} %shard_map.87), channel_id=1, source_target_pairs={{0,16},{1,17},{2,18},{3,19},{4,20},{5,21},{6,22},{7,23},{8,24},{9,... | collective-permute-start | bytes 442376 | tf_op jit(solution)/shard_map/ppermute | solution.py:278
  44.6 9.4 %collective-permute-done.7.enter_ref = bf16[144,512]{1,0:T(8,128)(2,1)S(1)} collective-permute-done((bf16[144,512]{1,0:T(8,128)(2,1)}, bf16[144,512]{1,0:T(8,128)(2,1)S(1)}, u32[]{:S(2)}, u32[]{:S(2)}) %collective-permute-start.7) | collective-permute-done | bytes 147488 | tf_op jit(solution)/shard_map/ppermute | solution.py:278
  53.9 0.6 copy-done.9
  54.6 1.8 %shard_map.88 = (bf16[128,512]{1,0:T(8,128)(2,1)}, bf16[128,512]{1,0:T(8,128)(2,1)}) custom-call(s32[5]{0:T(128)} %stack.23.ids, bf16[144,512]{1,0:T(8,128)(2,1)} %copy-done.9, bf16[144,512]{1,0:T(8,128)(2,1)} %get-tuple-element.35.own_ref, bf16[144,512]{1,0:T(8,128)(2,1)} %copy-done.5), custom_call_target="tpu_custom_call" | custom-call | flops 704512 | bytes 704512 | tf_op jit(solution)/shard_map/pallas_call | solution.py:263
  56.4 0.0 collective-permute-start.8
  56.4 4.0 %collective-permute-done.8.away_ref = bf16[128,512]{1,0:T(8,128)(2,1)S(1)} collective-permute-done((bf16[128,512]{1,0:T(8,128)(2,1)}, bf16[128,512]{1,0:T(8,128)(2,1)S(1)}, u32[]{:S(2)}, u32[]{:S(2)}) %collective-permute-start.8) | collective-permute-done | bytes 131104 | tf_op jit(solution)/shard_map/ppermute | solution.py:274
  60.4 0.6 copy-done.10
  61.1 2.9 %shard_map.89 = (bf16[128,1024]{1,0:T(8,128)(2,1)}, bf16[128,1024]{1,0:T(8,128)(2,1)}, bf16[128,1024]{1,0:T(8,128)(2,1)}, bf16[128,1024]{1,0:T(8,128)(2,1)}) custom-call(s32[5]{0:T(128)} %stack.23.ids, bf16[128,512]{1,0:T(8,128)(2,1)} %get-tuple-element.37.near_ref, bf16[128,512]{1,0:T(8,128)(2,1)} %copy-done.10, bf16[144,1024]{1,0:T(8,128)(2,1)} %get-tuple-element.31.p0, ...), custom_call_target="tpu_custom_call" | custom-call | flops 2490368 | bytes 2490368 | tf_op jit(solution)/shard_map/pallas_call | solution.py:263
  63.9 0.2 collective-permute-start.9
  64.1 0.3 collective-permute-start.10
  64.4 2.2 %collective-permute-start.11 = (bf16[128,1024]{1,0:T(8,128)(2,1)}, bf16[128,1024]{1,0:T(8,128)(2,1)S(1)}, u32[]{:S(2)}, u32[]{:S(2)}) collective-permute-start(bf16[128,1024]{1,0:T(8,128)(2,1)} %get-tuple-element.42), channel_id=1, source_target_pairs={{0,6},{1,7},{2,4},{3,5},{4,2},{5,3},{6,0},{7,1},{8,14},{9,15},{10,... | collective-permute-start | bytes 786440 | tf_op jit(solution)/shard_map/ppermute | solution.py:274
  66.6 3.6 %collective-permute-start = (f32[32]{0:T(128)S(1)}, f32[32]{0:T(128)S(1)}, u32[]{:S(2)}, u32[]{:S(2)}) collective-permute-start(f32[32]{0:T(128)S(1)} %copy-done.11), channel_id=1, source_target_pairs={{0,1},{1,0},{2,3},{3,2},{4,5},{5,4},{6,7},{7,6},{8,9},{9,8},{10,11... | collective-permute-start | bytes 392 | tf_op jit(solution)/shard_map/ppermute | solution.py:274
  70.2 0.8 collective-permute-done
  71.1 0.1 broadcast_select_fusion
  71.1 0.2 collective-permute-start.1
  71.3 0.0 collective-permute-done.9.s1
  71.3 0.0 collective-permute-done.10.s2
  71.4 0.0 copy-start.7
  71.4 4.1 %collective-permute-done.11.s3 = bf16[128,1024]{1,0:T(8,128)(2,1)S(1)} collective-permute-done((bf16[128,1024]{1,0:T(8,128)(2,1)}, bf16[128,1024]{1,0:T(8,128)(2,1)S(1)}, u32[]{:S(2)}, u32[]{:S(2)}) %collective-permute-start.11) | collective-permute-done | bytes 262176 | tf_op jit(solution)/shard_map/ppermute | solution.py:274
  75.4 0.7 copy-done.8
  76.1 3.6 %shard_map.90 = (bf16[4,128,1024]{2,1,0:T(8,128)(2,1)}, bf16[4,128,1024]{2,1,0:T(8,128)(2,1)}) custom-call(s32[5]{0:T(128)} %stack.23.ids, bf16[4,144,1024]{2,1,0:T(8,128)(2,1)} %shard_map.84.own_ref, bf16[4,144,1024]{2,1,0:T(8,128)(2,1)} %copy-done, bf16[128,1024]{1,0:T(8,128)(2,1)} %get-tuple-element.39.s0, bf16[128,1024]{1,0:T(8,128)(2,1)} %copy-done.6, ...), custom_call_target="tpu_custom_call" | custom-call | flops 5505024 | bytes 5505024 | tf_op jit(solution)/shard_map/pallas_call | solution.py:263
  79.8 4.2 %collective-permute-start.12 = (bf16[4,128,1024]{2,1,0:T(8,128)(2,1)}, bf16[4,128,1024]{2,1,0:T(8,128)(2,1)S(1)}, u32[]{:S(2)}, u32[]{:S(2)}) collective-permute-start(bf16[4,128,1024]{2,1,0:T(8,128)(2,1)} %get-tuple-element.43), channel_id=1, source_target_pairs={{0,1},{1,0},{2,3},{3,2},{4,5},{5,4},{6,7},{7,6},{8,9},{9,8},{10,11... | collective-permute-start | bytes 3145736 | tf_op jit(solution)/shard_map/ppermute | solution.py:274
  84.0 0.0 collective-permute-done.1
  84.0 0.6 broadcast_select_fusion.1.skip_ref
  84.6 12.8 %shard_map.83 = (f32[256,8192]{1,0:T(8,128)}, bf16[8,256,128]{2,1,0:T(8,128)(2,1)}) custom-call(bf16[256,8192]{1,0:T(8,128)(2,1)} %x_ref.5, bf16[256,8,128]{2,1,0:T(8,128)(2,1)} %c_ref.1, bf16[8,256,128]{2,1,0:T(8,128)(2,1)} %get-tuple-element.25.bg_ref, bf16[272,256]{1,0:T(8,128)(2,1)} %get-tuple-element.26.sx_ref.refs_2_, ...), custom_call_target="tpu_custom_call" | custom-call | flops 10000000000 | bytes 16777216 | tf_op jit(solution)/shard_map/pallas_call | solution.py:397
  97.4 8.4 %shard_map.91.refs_7_ = bf16[256,8192]{1,0:T(8,128)(2,1)} custom-call(s32[5]{0:T(128)} %stack.23.ids, f32[256,8192]{1,0:T(8,128)} %get-tuple-element.28.refs_0_, bf16[8,256,128]{2,1,0:T(8,128)(2,1)} %get-tuple-element.29.refs_1_, bf16[272,256]{1,0:T(8,128)(2,1)} %get-tuple-element.26.sx_ref.refs_2_, bf16[256,256]{1,0:T(8,128)(2,1)} %get-tuple-element.27.sr_ref.refs_3_, ...), custom_call_target="tpu_custom_call" | custom-call | flops 1000000000 | bytes 10485760 | tf_op jit(solution)/shard_map/pallas_call | solution.py:454
  105.8 0.0 collective-permute-done.12.refs_4_
  105.8 1.0 copy-done.4
  106.8 8.4 %shard_map.92 = bf16[256,8192]{1,0:T(8,128)(2,1)} custom-call(s32[5]{0:T(128)} %stack.23.ids, f32[256,8192]{1,0:T(8,128)} %get-tuple-element.28.refs_0_, bf16[8,256,128]{2,1,0:T(8,128)(2,1)} %get-tuple-element.29.refs_1_, bf16[272,256]{1,0:T(8,128)(2,1)} %get-tuple-element.26.sx_ref.refs_2_, ...), custom_call_target="tpu_custom_call", output_to_operand_aliasing={{}: (8, {})} | custom-call | flops 1000000000 | bytes 10485760 | tf_op jit(solution)/shard_map/pallas_call | solution.py:462
  (16 shorter events, 0.0 us)
Async XLA Ops:
  7.0 6.5 %collective-permute-start.2 = (bf16[4,144,1024]{2,1,0:T(8,128)(2,1)}, bf16[4,144,1024]{2,1,0:T(8,128)(2,1)S(1)}, u32[]{:S(2)}, u32[]{:S(2)}) collective-permute-start(bf16[4,144,1024]{2,1,0:T(8,128)(2,1)} %get-tuple-element.30), channel_id=1, source_target_pairs={{0,1},{1,0},{2,3},{3,2},{4,5},{5,4},{6,7},{7,6},{8,9},{9,8},{10,11... | collective-permute-start | bytes 3538952 | tf_op jit(solution)/shard_map/ppermute | solution.py:274
  13.5 53.1 %copy-start.11 = (f32[32]{0:T(128)S(1)}, f32[32]{0:T(128)}, u32[]{:S(2)}) copy-start(f32[32]{0:T(128)} %param.14) | copy-start | bytes 388
  13.5 1.0 copy-start
  17.6 8.8 %collective-permute-start.3 = (bf16[144,1024]{1,0:T(8,128)(2,1)}, bf16[144,1024]{1,0:T(8,128)(2,1)S(1)}, u32[]{:S(2)}, u32[]{:S(2)}) collective-permute-start(bf16[144,1024]{1,0:T(8,128)(2,1)} %get-tuple-element.32), channel_id=1, source_target_pairs={{0,2},{1,3},{2,0},{3,1},{4,6},{5,7},{6,4},{7,5},{8,10},{9,11},{10,... | collective-permute-start | bytes 884744 | tf_op jit(solution)/shard_map/ppermute | solution.py:274
  17.8 8.5 %collective-permute-start.4 = (bf16[144,1024]{1,0:T(8,128)(2,1)}, bf16[144,1024]{1,0:T(8,128)(2,1)S(1)}, u32[]{:S(2)}, u32[]{:S(2)}) collective-permute-start(bf16[144,1024]{1,0:T(8,128)(2,1)} %get-tuple-element.33), channel_id=1, source_target_pairs={{0,4},{1,5},{2,6},{3,7},{4,0},{5,1},{6,2},{7,3},{8,12},{9,13},{10,... | collective-permute-start | bytes 884744 | tf_op jit(solution)/shard_map/ppermute | solution.py:274
  18.0 15.5 %collective-permute-start.5 = (bf16[144,1024]{1,0:T(8,128)(2,1)}, bf16[144,1024]{1,0:T(8,128)(2,1)S(1)}, u32[]{:S(2)}, u32[]{:S(2)}) collective-permute-start(bf16[144,1024]{1,0:T(8,128)(2,1)} %get-tuple-element.34), channel_id=1, source_target_pairs={{0,6},{1,7},{2,4},{3,5},{4,2},{5,3},{6,0},{7,1},{8,14},{9,15},{10,... | collective-permute-start | bytes 884744 | tf_op jit(solution)/shard_map/ppermute | solution.py:274
  26.3 7.2 %copy-start.1 = (bf16[144,1024]{1,0:T(8,128)(2,1)}, bf16[144,1024]{1,0:T(8,128)(2,1)S(1)}, u32[]{:S(2)}) copy-start(bf16[144,1024]{1,0:T(8,128)(2,1)S(1)} %collective-permute-done.3.p1) | copy-start | bytes 884740
  26.3 7.2 %copy-start.2 = (bf16[144,1024]{1,0:T(8,128)(2,1)}, bf16[144,1024]{1,0:T(8,128)(2,1)S(1)}, u32[]{:S(2)}) copy-start(bf16[144,1024]{1,0:T(8,128)(2,1)S(1)} %collective-permute-done.4.p2) | copy-start | bytes 884740
  33.6 0.7 copy-start.3
  36.7 4.2 %collective-permute-start.6 = (bf16[144,512]{1,0:T(8,128)(2,1)}, bf16[144,512]{1,0:T(8,128)(2,1)S(1)}, u32[]{:S(2)}, u32[]{:S(2)}) collective-permute-start(bf16[144,512]{1,0:T(8,128)(2,1)} %get-tuple-element.36), channel_id=1, source_target_pairs={{0,8},{1,9},{2,10},{3,11},{4,12},{5,13},{6,14},{7,15},{8,0},{9,1},... | collective-permute-start | bytes 442376 | tf_op jit(solution)/shard_map/ppermute | solution.py:274
  40.9 0.7 copy-start.5
  43.3 10.7 %collective-permute-start.7 = (bf16[144,512]{1,0:T(8,128)(2,1)}, bf16[144,512]{1,0:T(8,128)(2,1)S(1)}, u32[]{:S(2)}, u32[]{:S(2)}) collective-permute-start(bf16[144,512]{1,0:T(8,128)(2,1)} %shard_map.87), channel_id=1, source_target_pairs={{0,16},{1,17},{2,18},{3,19},{4,20},{5,21},{6,22},{7,23},{8,24},{9,... | collective-permute-start | bytes 442376 | tf_op jit(solution)/shard_map/ppermute | solution.py:278
  53.9 0.6 copy-start.9
  56.4 4.0 %collective-permute-start.8 = (bf16[128,512]{1,0:T(8,128)(2,1)}, bf16[128,512]{1,0:T(8,128)(2,1)S(1)}, u32[]{:S(2)}, u32[]{:S(2)}) collective-permute-start(bf16[128,512]{1,0:T(8,128)(2,1)} %get-tuple-element.38), channel_id=1, source_target_pairs={{0,8},{1,9},{2,10},{3,11},{4,12},{5,13},{6,14},{7,15},{8,0},{9,1},... | collective-permute-start | bytes 393224 | tf_op jit(solution)/shard_map/ppermute | solution.py:274
  60.4 0.7 copy-start.10
  63.9 7.4 %collective-permute-start.9 = (bf16[128,1024]{1,0:T(8,128)(2,1)}, bf16[128,1024]{1,0:T(8,128)(2,1)S(1)}, u32[]{:S(2)}, u32[]{:S(2)}) collective-permute-start(bf16[128,1024]{1,0:T(8,128)(2,1)} %get-tuple-element.40), channel_id=1, source_target_pairs={{0,2},{1,3},{2,0},{3,1},{4,6},{5,7},{6,4},{7,5},{8,10},{9,11},{10,... | collective-permute-start | bytes 786440 | tf_op jit(solution)/shard_map/ppermute | solution.py:274
  64.1 7.2 %collective-permute-start.10 = (bf16[128,1024]{1,0:T(8,128)(2,1)}, bf16[128,1024]{1,0:T(8,128)(2,1)S(1)}, u32[]{:S(2)}, u32[]{:S(2)}) collective-permute-start(bf16[128,1024]{1,0:T(8,128)(2,1)} %get-tuple-element.41), channel_id=1, source_target_pairs={{0,4},{1,5},{2,6},{3,7},{4,0},{5,1},{6,2},{7,3},{8,12},{9,13},{10,... | collective-permute-start | bytes 786440 | tf_op jit(solution)/shard_map/ppermute | solution.py:274
  64.4 11.0 %collective-permute-start.11 = (bf16[128,1024]{1,0:T(8,128)(2,1)}, bf16[128,1024]{1,0:T(8,128)(2,1)S(1)}, u32[]{:S(2)}, u32[]{:S(2)}) collective-permute-start(bf16[128,1024]{1,0:T(8,128)(2,1)} %get-tuple-element.42), channel_id=1, source_target_pairs={{0,6},{1,7},{2,4},{3,5},{4,2},{5,3},{6,0},{7,1},{8,14},{9,15},{10,... | collective-permute-start | bytes 786440 | tf_op jit(solution)/shard_map/ppermute | solution.py:274
  66.6 4.5 %collective-permute-start = (f32[32]{0:T(128)S(1)}, f32[32]{0:T(128)S(1)}, u32[]{:S(2)}, u32[]{:S(2)}) collective-permute-start(f32[32]{0:T(128)S(1)} %copy-done.11), channel_id=1, source_target_pairs={{0,1},{1,0},{2,3},{3,2},{4,5},{5,4},{6,7},{7,6},{8,9},{9,8},{10,11... | collective-permute-start | bytes 392 | tf_op jit(solution)/shard_map/ppermute | solution.py:274
  71.1 12.9 %collective-permute-start.1 = (f32[64]{0:T(128)S(1)}, f32[64]{0:T(128)S(1)}, u32[]{:S(2)}, u32[]{:S(2)}) collective-permute-start(f32[64]{0:T(128)S(1)} %broadcast_select_fusion), channel_id=1, source_target_pairs={{0,2},{1,3},{2,0},{3,1},{4,6},{5,7},{6,4},{7,5},{8,10},{9,11},{10,... | collective-permute-start | bytes 776 | tf_op jit(solution)/shard_map/ppermute | solution.py:274
  71.3 4.1 %copy-start.6 = (bf16[128,1024]{1,0:T(8,128)(2,1)}, bf16[128,1024]{1,0:T(8,128)(2,1)S(1)}, u32[]{:S(2)}) copy-start(bf16[128,1024]{1,0:T(8,128)(2,1)S(1)} %collective-permute-done.9.s1) | copy-start | bytes 786436
  71.4 4.1 %copy-start.7 = (bf16[128,1024]{1,0:T(8,128)(2,1)}, bf16[128,1024]{1,0:T(8,128)(2,1)S(1)}, u32[]{:S(2)}) copy-start(bf16[128,1024]{1,0:T(8,128)(2,1)S(1)} %collective-permute-done.10.s2) | copy-start | bytes 786436
  75.4 0.7 copy-start.8
  79.8 26.0 %collective-permute-start.12 = (bf16[4,128,1024]{2,1,0:T(8,128)(2,1)}, bf16[4,128,1024]{2,1,0:T(8,128)(2,1)S(1)}, u32[]{:S(2)}, u32[]{:S(2)}) collective-permute-start(bf16[4,128,1024]{2,1,0:T(8,128)(2,1)} %get-tuple-element.43), channel_id=1, source_target_pairs={{0,1},{1,0},{2,3},{3,2},{4,5},{5,4},{6,7},{7,6},{8,9},{9,8},{10,11... | collective-permute-start | bytes 3145736 | tf_op jit(solution)/shard_map/ppermute | solution.py:274
  105.8 1.0 copy-start.4
